TPU v7x, 32 devices: a whole 2x2x4 slice. The times are simulated.
32 devices in a mesh: dec: 2 (over x), ada: 16 (over z, y, core).
Axes of the slice: x: 2, y: 2, z: 4, core: 2. Of those that a mesh axis runs over, the one named last changes fastest.
Arguments:
- inputs: bfloat16 [4, 64, 8192], P(None, ('dec', 'ada')), may hold values from -6 to 6
- query_weight: bfloat16 [8192, 8192], P(None, 'ada'), may hold values from -0.0625 to 0.0625
- adapter_down: bfloat16 [32, 8192, 64], P(('dec', 'ada')), may hold values from -0.0625 to 0.0625
- adapter_up: bfloat16 [32, 64, 8192], P(('dec', 'ada')), may hold values from -0.75 to 0.75
- adapter_ids: int32 [64, 1], P(('dec', 'ada')), may hold values from 0 to 15; in each aligned block of 32 rows (0 to 31, 32 to 63, ...) at most 4 rows name the same one
- new_cache: bfloat16 [4, 64, 2, 1024], P(None, ('dec', 'ada')), may hold values from -9 to 9
- cache_pool: bfloat16 [256, 2, 16, 1024], P(('dec', 'ada')), may hold values from -400 to 400
- page_table: int32 [64, 4], P(('dec', 'ada')), may hold values from 0 to 15, as said below
- lengths: int32 [64], P(('dec', 'ada')), may hold values from 1 to 64, as said below
Outputs:
- attended: bfloat16 [4, 64, 8192], P(None, ('dec', 'ada'))
Inputs may be any that keep to these rules, and one draw needn't show every extreme that they name: `adapter_ids`: in each aligned block of 32 rows (one decode group) no id is named by more than 4 rows, a bound that some block reaches. `page_table`: entries j >= ceil(lengths[r] / 16) are unused. Among rows with the same (r % 32) // 2, the live entries are all different. `lengths`: among rows with the same (r % 32) // 2, one reaches 64.
All inputs are finite; a program needn't handle non-finite values.
Results may differ from a plain program's by a relative error of at most 0.007.
The roundings to bfloat16 on the way count: a program that leaves them out, or rounds other values in their place, can miss the bound.
Values may be sent and summed in bfloat16 or wider, within the bound.
A program may use at most 64 MiB of HBM per device.

v0:
```python
import math
import jax
import jax.numpy as jnp
from jax import lax
from jax.sharding import PartitionSpec as P

HEADS = 64
KVH = 8
HD = 128
CAP = 4
NEGATIVE = -1e30
HIGH = lax.Precision.HIGHEST


def cache_part(query, keys, values, live):
    scale = 1.0 / math.sqrt(query.shape[-1])
    scores = (
        jnp.einsum("trkgd,rpkd->trkgp", query, keys, preferred_element_type=jnp.float32) * scale
    )
    mask = live[None, :, None, None, :]
    scores = jnp.where(mask, scores, NEGATIVE)
    top = jnp.max(scores, axis=-1)
    weights = jnp.where(mask, jnp.exp(scores - top[..., None]), 0.0)
    numerator = jnp.einsum("trkgp,rpkd->trkgd", weights, values.astype(jnp.float32), precision=HIGH)
    return (numerator, top, jnp.sum(weights, axis=-1))


def fresh_part(query, new_entries):
    steps, rows, kv_heads, group, head_dim = query.shape
    scale = 1.0 / math.sqrt(head_dim)
    keys = new_entries[:, :, 0].reshape(new_entries.shape[0], rows, kv_heads, head_dim)
    values = new_entries[:, :, 1].reshape(new_entries.shape[0], rows, kv_heads, head_dim)
    scores = (
        jnp.einsum("trkgd,urkd->trkgu", query, keys, preferred_element_type=jnp.float32) * scale
    )
    allowed = (jnp.arange(new_entries.shape[0])[None, :] <= jnp.arange(steps)[:, None])[
        :, None, None, None, :
    ]
    scores = jnp.where(allowed, scores, NEGATIVE)
    top = jnp.max(scores, axis=-1)
    weights = jnp.where(allowed, jnp.exp(scores - top[..., None]), 0.0)
    numerator = jnp.einsum("trkgu,urkd->trkgd", weights, values.astype(jnp.float32), precision=HIGH)
    return (numerator, top, jnp.sum(weights, axis=-1))


def body(
    inputs,
    query_weight,
    adapter_down,
    adapter_up,
    adapter_ids,
    new_cache,
    cache_pool,
    page_table,
    lengths,
):
    steps, row_local, width = inputs.shape
    adapter_total_count = lax.axis_size("ada")
    dec_count = lax.axis_size("dec")
    head_cols = query_weight.shape[1]
    held_adapters = adapter_down.shape[0]
    adapter_rank = adapter_down.shape[2]
    group = row_local * adapter_total_count
    capacity = CAP
    slots = held_adapters * capacity
    whole_inputs, group_ids = (
        lax.all_gather(inputs, "ada", axis=1, tiled=True),
        lax.all_gather(adapter_ids, "ada", axis=0, tiled=True),
    )
    base_output = jnp.dot(
        whole_inputs.reshape(steps * group, width), query_weight, preferred_element_type=jnp.float32
    )
    base_output = base_output.reshape(steps, group, head_cols)
    row_adapter = group_ids[:, 0]
    order = jnp.arange(group)
    earlier = (row_adapter[:, None] == row_adapter[None, :]) & (order[None, :] < order[:, None])
    earlier_count = jnp.sum(earlier.astype(jnp.int32), axis=1)
    slot_of_row = (
        row_adapter // held_adapters * slots
        + row_adapter % held_adapters * capacity
        + earlier_count
    )
    local_slot = slot_of_row - lax.axis_index("ada") * slots
    pick = (local_slot[None, :] == jnp.arange(slots)[:, None]).astype(jnp.bfloat16)
    chosen = jnp.einsum(
        "sg,tgd->tsd", pick, whole_inputs, preferred_element_type=jnp.float32
    ).astype(jnp.bfloat16)
    chosen = chosen.reshape(steps, held_adapters, capacity, width)
    shrink = jnp.einsum(
        "tjcd,jdr->tjcr", chosen, adapter_down, preferred_element_type=jnp.float32
    ).astype(jnp.bfloat16)
    columns = lax.all_to_all(adapter_up, "ada", split_axis=2, concat_axis=0, tiled=True)
    every_shrink = lax.all_gather(
        shrink.reshape(steps, slots, adapter_rank), "ada", axis=1, tiled=True
    )
    every_shrink = every_shrink.reshape(
        steps, adapter_total_count * held_adapters, capacity, adapter_rank
    )
    received_rows = jnp.einsum(
        "tacr,arh->tach", every_shrink, columns, preferred_element_type=jnp.float32
    ).astype(jnp.bfloat16)
    received_rows = received_rows.reshape(steps, adapter_total_count * slots, head_cols)
    slot_position = (
        slot_of_row[:, None] == jnp.arange(adapter_total_count * slots)[None, :]
    ).astype(jnp.bfloat16)
    low_rank_update = jnp.einsum(
        "mr,urx->umx", slot_position, received_rows, preferred_element_type=jnp.float32
    )
    query_columns = (base_output + low_rank_update).astype(jnp.bfloat16)
    query_local = lax.all_to_all(query_columns, "ada", split_axis=1, concat_axis=2, tiled=True)
    group_heads = HEADS // KVH
    query = query_local.reshape(steps, row_local, KVH, group_heads, HD)
    fresh = fresh_part(query, new_cache)
    pool_local = cache_pool.shape[0]
    page_length = cache_pool.shape[2]
    table_width = page_table.shape[1]
    position = jnp.arange(table_width * page_length)
    every_query, every_table, every_length = (
        lax.all_gather(query_local, "dec", axis=1, tiled=True),
        lax.all_gather(page_table, "dec", axis=0, tiled=True),
        lax.all_gather(lengths, "dec", axis=0, tiled=True),
    )
    column_rows = dec_count * row_local
    asked = every_query.reshape(steps, column_rows, KVH, group_heads, HD)
    local = every_table // pool_local == lax.axis_index("dec")
    pages = cache_pool[every_table % pool_local]
    keys = pages[:, :, 0].reshape(column_rows, table_width * page_length, KVH, HD)
    values = pages[:, :, 1].reshape(column_rows, table_width * page_length, KVH, HD)
    live = (position[None, :] < every_length[:, None]) & jnp.repeat(local, page_length, axis=1)
    partial_numerator, part_top, part_total = cache_part(asked, keys, values, live)
    partial_numerator = partial_numerator.reshape(steps, dec_count, row_local, KVH, group_heads, HD)
    part_top = part_top.reshape(steps, dec_count, row_local, KVH, group_heads)
    part_total = part_total.reshape(steps, dec_count, row_local, KVH, group_heads)
    back_numerator, back_top, back_total = (
        lax.all_to_all(partial_numerator, "dec", split_axis=1, concat_axis=1, tiled=True),
        lax.all_to_all(part_top, "dec", split_axis=1, concat_axis=1, tiled=True),
        lax.all_to_all(part_total, "dec", split_axis=1, concat_axis=1, tiled=True),
    )
    top = jnp.maximum(jnp.max(back_top, axis=1), fresh[1])
    factor = jnp.exp(back_top - top[:, None])
    numerator = (
        jnp.sum(back_numerator * factor[..., None], axis=1)
        + fresh[0] * jnp.exp(fresh[1] - top)[..., None]
    )
    total = jnp.sum(back_total * factor, axis=1) + fresh[2] * jnp.exp(fresh[1] - top)
    attended = (numerator / total[..., None]).astype(jnp.bfloat16)
    return attended.reshape(steps, row_local, width)


def solution(mesh):
    in_specs = (
        P(None, ("dec", "ada"), None),
        P(None, "ada"),
        P(("dec", "ada"), None, None),
        P(("dec", "ada"), None, None),
        P(("dec", "ada"), None),
        P(None, ("dec", "ada"), None, None),
        P(("dec", "ada"), None, None, None),
        P(("dec", "ada"), None),
        P(("dec", "ada")),
    )
    out_specs = P(None, ("dec", "ada"), None)
    return jax.shard_map(body, mesh=mesh, in_specs=in_specs, out_specs=out_specs, check_vma=False)
```

profile of v0, /device:TPU:0, one launch (start us, length us, event | category | flops | bytes accessed | tf_op | source)
XLA Modules:
  0.0 197.2 jit_solution(16430546696477317186)
XLA Ops:
  6.5 1.8 copy.73
  8.3 0.0 all-gather.3.cloned.1.call-update
  8.3 9.2 %copy.78 = bf16[1,64,8192]{1,0,2:T(2,128)(2,1)} copy(bf16[1,64,8192]{2,1,0:T(8,128)(2,1)} %param.12) | data formatting | bytes 2097152 | tf_op args[3]
  17.5 0.5 broadcast.160
  18.0 45.2 %reduce.4 = bf16[8192,64]{1,0:T(8,128)(2,1)S(1)} reduce(bf16[8192,1,64]{2,1,0:T(2,128)(2,1)} %bitcast.122, bf16[]{:T(256)} %broadcast.160), dimensions={1}, to_apply=%bitcast.103.reduce_sub_computation | reduce | bytes 2097154
  63.2 0.0 copy-start.8
  63.2 2.3 %reshape.164 = bf16[16,2,16384]{2,1,0:T(2,128)(2,1)} reshape(bf16[8192,64]{1,0:T(8,128)(2,1)S(1)} %reduce.4) | data formatting | bytes 2097152
  65.5 7.4 %all-to-all-start = ((bf16[16,2,16384]{2,1,0:T(2,128)(2,1)}), bf16[16,2,16384]{2,1,0:T(2,128)(2,1)S(1)}, u32[]{:S(2)}, u32[]{:S(2)}) async-start(bf16[16,2,16384]{2,1,0:T(2,128)(2,1)} %reshape.164), calls=%async_computation | async-start | bytes 2097152 | tf_op jit(solution)/shard_map/all_to_all | solution.py:92
  72.9 4.2 %all-gather = s32[2,2,4]{2,1,0:T(2,128)S(1)} all-gather(s32[1,2,4]{2,1,0:T(2,128)S(1)} %bitcast.148), channel_id=1, replica_groups=mesh['dec'=2,'ada'=16] {'dec'}, dimensions={0}, use_global_device_ids=true | all-gather | bytes 96 | tf_op jit(solution)/shard_map/all_gather | solution.py:120
  77.2 0.7 dynamic-slice
  78.6 0.2 dynamic-update-slice
  78.8 4.3 %all-reduce = s32[4]{0:T(128)S(1)} all-reduce(s32[4]{0:T(128)S(1)} %dynamic-update-slice), channel_id=1, replica_groups=mesh['dec'=2,'ada'=16] {'dec'}, use_global_device_ids=true, to_apply=%add | all-reduce | flops 4 | bytes 32
  83.1 0.7 dynamic-slice.1
  84.4 0.1 reshape.126
  84.5 0.1 broadcast_in_dim.65
  84.6 0.1 reshape.114
  84.7 0.2 slice_reduce_fusion
  84.9 1.7 gather_fusion
  86.6 0.1 fusion.55
  86.7 0.1 copy.119
  86.8 0.9 copy.118
  87.7 0.1 bitcast_dynamic-update-slice_fusion
  87.8 12.3 %all-reduce.1 = s32[32]{0:T(128)S(1)} all-reduce(s32[32]{0:T(128)S(1)} %bitcast_dynamic-update-slice_fusion), channel_id=1, replica_groups=mesh['dec'=2,'ada'=16] {'ada'}, use_global_device_ids=true, to_apply=%add.1 | all-reduce | flops 32 | bytes 256 | tf_op jit(solution)/shard_map/squeeze | solution.py:74
  100.2 0.2 convert_reduce_fusion
  100.4 0.1 fusion.46
  100.4 0.9 bitcast_bitcast_fusion
  101.3 7.0 %reshape.165 = bf16[8192,1,64]{2,1,0:T(2,128)(2,1)} reshape(bf16[16,2,16384]{2,1,0:T(2,128)(2,1)S(1)} %all-to-all-done) | data formatting | bytes 2097152
  108.3 2.5 %copy.115 = bf16[1,64,8192]{1,2,0:T(8,128)(2,1)S(1)} copy(bf16[1,64,8192]{1,0,2:T(2,128)(2,1)} %bitcast.123) | data formatting | bytes 2097152
  110.8 1.6 copy.80
  112.4 4.4 %fusion.19 = bf16[4,4,64]{2,1,0:T(4,128)(2,1)S(1)} fusion(bf16[4,32,8192]{2,0,1:T(4,128)(2,1)} %all-gather.3.cloned.1.call-done, bf16[1,8192,64]{1,2,0:T(8,128)(2,1)S(1)} %copy-done, s32[32]{0:T(128)S(1)} %get-tuple-element.11), kind=kOutput, calls=%fused_computation.24 | convolution fusion | flops 25298048 | bytes 3147904 | tf_op jit(solution)/shard_map/tjcd,jdr->tjcr/dot_general | solution.py:89
  116.8 19.0 %all_gather.22 = bf16[4,64,64]{2,0,1:T(4,128)(2,1)S(1)} all-gather(bf16[4,4,64]{2,0,1:T(4,128)(2,1)S(1)} %copy.76), channel_id=1, replica_groups=mesh['dec'=2,'ada'=16] {'ada'}, dimensions={1}, use_global_device_ids=true | all-gather | bytes 34816 | tf_op jit(solution)/shard_map/all_gather | solution.py:93
  135.8 1.5 fusion.7
  137.3 0.1 copy.82
  137.4 5.7 %fusion.1 = f32[4,32,512]{2,1,0:T(8,128)S(1)} fusion(bf16[8192,512]{1,0:T(8,128)(2,1)} %param.10, bf16[4,32,8192]{2,0,1:T(4,128)(2,1)S(1)} %copy-done.1), kind=kOutput, calls=%fused_computation.3 | convolution fusion | flops 1073741824 | bytes 10747904 | tf_op jit(solution)/shard_map/dot_general | solution.py:70
  143.2 0.2 fusion.15
  143.4 0.8 copy.84
  144.1 3.5 %all-to-all-start.1 = ((bf16[4,32,512]{2,0,1:T(4,128)(2,1)}), bf16[4,32,512]{2,0,1:T(4,128)(2,1)S(1)}, u32[]{:S(2)}, u32[]{:S(2)}) async-start(bf16[4,32,512]{2,0,1:T(4,128)(2,1)} %copy.84), calls=%async_computation.1 | async-start | bytes 262144 | tf_op jit(solution)/shard_map/all_to_all | solution.py:110
  147.7 1.1 bitcast_bitcast_fusion.1
  148.8 6.8 %all-to-all-done.1 = bf16[4,32,512]{2,0,1:T(4,128)(2,1)S(1)} async-done(((bf16[4,32,512]{2,0,1:T(4,128)(2,1)}), bf16[4,32,512]{2,0,1:T(4,128)(2,1)S(1)}, u32[]{:S(2)}, u32[]{:S(2)}) %all-to-all-start.1) | async-done | bytes 131104 | tf_op jit(solution)/shard_map/all_to_all | solution.py:110
  155.6 0.1 reshape.121
  155.7 0.1 all_to_all.42
  155.8 5.6 %all_gather.23 = bf16[4,4,8192]{2,0,1:T(4,128)(2,1)S(1)} all-gather(bf16[4,2,8192]{2,0,1:T(4,128)(2,1)S(1)} %all_to_all.42), channel_id=1, replica_groups=mesh['dec'=2,'ada'=16] {'dec'}, dimensions={1}, use_global_device_ids=true | all-gather | bytes 393216 | tf_op jit(solution)/shard_map/all_gather | solution.py:119
  161.4 0.3 reshape.161
  161.7 0.5 fusion.56
  162.2 0.4 fusion.27
  162.7 1.5 fusion.25
  164.1 0.7 reshape.166
  164.9 3.2 %all-to-all-start.3 = ((f32[2,1,512]{2,1,0:T(1,128)}), f32[2,1,512]{2,1,0:T(1,128)S(1)}, u32[]{:S(2)}, u32[]{:S(2)}) async-start(f32[2,1,512]{2,1,0:T(1,128)} %reshape.166), calls=%async_computation.3 | async-start | bytes 8192 | tf_op jit(solution)/shard_map/all_to_all | solution.py:136
  168.1 0.7 fusion.57
  168.8 0.2 fusion.34
  169.0 0.7 reshape.168
  169.7 2.2 %all-to-all-done.3 = f32[2,1,512]{2,1,0:T(1,128)S(1)} async-done(((f32[2,1,512]{2,1,0:T(1,128)}), f32[2,1,512]{2,1,0:T(1,128)S(1)}, u32[]{:S(2)}, u32[]{:S(2)}) %all-to-all-start.3) | async-done | bytes 4128 | tf_op jit(solution)/shard_map/all_to_all | solution.py:136
  171.9 3.2 %all-to-all-start.4 = ((f32[2,1,512]{2,1,0:T(1,128)}), f32[2,1,512]{2,1,0:T(1,128)S(1)}, u32[]{:S(2)}, u32[]{:S(2)}) async-start(f32[2,1,512]{2,1,0:T(1,128)} %reshape.168), calls=%async_computation.4 | async-start | bytes 8192 | tf_op jit(solution)/shard_map/all_to_all | solution.py:137
  175.1 0.5 broadcast.161
  175.6 0.7 reduce.5
  176.3 0.1 reshape.167
  176.4 2.4 %all-to-all-done.4 = f32[2,1,512]{2,1,0:T(1,128)S(1)} async-done(((f32[2,1,512]{2,1,0:T(1,128)}), f32[2,1,512]{2,1,0:T(1,128)S(1)}, u32[]{:S(2)}, u32[]{:S(2)}) %all-to-all-start.4) | async-done | bytes 4128 | tf_op jit(solution)/shard_map/all_to_all | solution.py:137
  178.9 3.5 %all-to-all-start.2 = ((f32[4,2,2,8,8,128]{5,4,0,3,2,1:T(8,128)}), f32[4,2,2,8,8,128]{5,4,0,3,2,1:T(8,128)S(1)}, u32[]{:S(2)}, u32[]{:S(2)}) async-start(f32[4,2,2,8,8,128]{5,4,0,3,2,1:T(8,128)} %bitcast.27), calls=%async_computation.2 | async-start | bytes 1048576 | tf_op jit(solution)/shard_map/all_to_all | solution.py:135
  182.4 0.7 reduce.6
  183.0 0.1 reshape.169
  183.2 5.7 %all-to-all-done.2 = f32[4,2,2,8,8,128]{5,4,0,3,2,1:T(8,128)S(1)} async-done(((f32[4,2,2,8,8,128]{5,4,0,3,2,1:T(8,128)}), f32[4,2,2,8,8,128]{5,4,0,3,2,1:T(8,128)S(1)}, u32[]{:S(2)}, u32[]{:S(2)}) %all-to-all-start.2) | async-done | bytes 524320 | tf_op jit(solution)/shard_map/all_to_all | solution.py:135
  188.9 0.2 multiply_reduce_fusion
  189.1 0.5 fusion.16
  189.7 0.7 reshape.123
  (37 shorter events, 0.4 us)
Async XLA Ops:
  6.5 105.9 %copy-start = (bf16[1,8192,64]{1,2,0:T(8,128)(2,1)S(1)}, bf16[1,8192,64]{1,2,0:T(8,128)(2,1)}, u32[]{:S(2)}) copy-start(bf16[1,8192,64]{1,2,0:T(8,128)(2,1)} %param.11) | copy-start | bytes 3145732
  6.5 105.9 %all-gather.3.cloned.1.call-start = ((), (), s32[]{:S(2)}) async-start(), calls=%async_computation.5 | async-start | bytes 2228224 | tf_op jit(solution)/shard_map/all_gather | solution.py:67
  63.2 9.8 %copy-start.4 = (s32[2,4]{1,0:T(2,128)S(1)}, s32[2,4]{1,0:T(2,128)}, u32[]{:S(2)}) copy-start(s32[2,4]{1,0:T(2,128)} %param.16) | copy-start | bytes 100
  63.2 14.0 %copy-start.8 = (u32[32]{0:T(128)S(1)}, u32[32]{0:T(128)}, u32[]{:S(2)}) copy-start(u32[32]{0:T(128)} %constant.88) | copy-start | bytes 388
  63.2 15.4 %copy-start.5 = (s32[2]{0:T(128)S(1)}, s32[2]{0:T(128)}, u32[]{:S(2)}) copy-start(s32[2]{0:T(128)} %param.17) | copy-start | bytes 28
  63.2 19.9 %copy-start.7 = (u32[32]{0:T(128)S(1)}, u32[32]{0:T(128)}, u32[]{:S(2)}) copy-start(u32[32]{0:T(128)} %constant.93) | copy-start | bytes 388
  63.2 21.5 %copy-start.3 = (bf16[4,2,2,1024]{3,2,1,0:T(2,128)(2,1)S(1)}, bf16[4,2,2,1024]{3,2,1,0:T(2,128)(2,1)}, u32[]{:S(2)}) copy-start(bf16[4,2,2,1024]{3,2,1,0:T(2,128)(2,1)} %param.14) | copy-start | bytes 98308
  65.5 35.8 %all-to-all-start = ((bf16[16,2,16384]{2,1,0:T(2,128)(2,1)}), bf16[16,2,16384]{2,1,0:T(2,128)(2,1)S(1)}, u32[]{:S(2)}, u32[]{:S(2)}) async-start(bf16[16,2,16384]{2,1,0:T(2,128)(2,1)} %reshape.164), calls=%async_computation | async-start | bytes 2097152 | tf_op jit(solution)/shard_map/all_to_all | solution.py:92
  86.6 1.1 copy-start.6
  112.4 25.0 %copy-start.1 = (bf16[4,32,8192]{2,0,1:T(4,128)(2,1)S(1)}, bf16[4,32,8192]{2,0,1:T(4,128)(2,1)}, u32[]{:S(2)}) copy-start(bf16[4,32,8192]{2,0,1:T(4,128)(2,1)} %all-gather.3.cloned.1.call-done) | copy-start | bytes 6291460
  143.1 18.6 %copy-start.2 = (bf16[4,64,8,128,1]{3,2,1,0,4:T(8,128)(2,1)S(1)}, bf16[4,64,8,128,1]{3,2,1,0,4:T(8,128)(2,1)}, u32[]{:S(2)}) copy-start(bf16[4,64,8,128,1]{3,2,1,0,4:T(8,128)(2,1)} %bitcast_bitcast_fusion) | copy-start | bytes 1572868
  144.1 11.4 %all-to-all-start.1 = ((bf16[4,32,512]{2,0,1:T(4,128)(2,1)}), bf16[4,32,512]{2,0,1:T(4,128)(2,1)S(1)}, u32[]{:S(2)}, u32[]{:S(2)}) async-start(bf16[4,32,512]{2,0,1:T(4,128)(2,1)} %copy.84), calls=%async_computation.1 | async-start | bytes 262144 | tf_op jit(solution)/shard_map/all_to_all | solution.py:110
  164.9 7.0 %all-to-all-start.3 = ((f32[2,1,512]{2,1,0:T(1,128)}), f32[2,1,512]{2,1,0:T(1,128)S(1)}, u32[]{:S(2)}, u32[]{:S(2)}) async-start(f32[2,1,512]{2,1,0:T(1,128)} %reshape.166), calls=%async_computation.3 | async-start | bytes 8192 | tf_op jit(solution)/shard_map/all_to_all | solution.py:136
  171.9 7.0 %all-to-all-start.4 = ((f32[2,1,512]{2,1,0:T(1,128)}), f32[2,1,512]{2,1,0:T(1,128)S(1)}, u32[]{:S(2)}, u32[]{:S(2)}) async-start(f32[2,1,512]{2,1,0:T(1,128)} %reshape.168), calls=%async_computation.4 | async-start | bytes 8192 | tf_op jit(solution)/shard_map/all_to_all | solution.py:137
  178.9 10.1 %all-to-all-start.2 = ((f32[4,2,2,8,8,128]{5,4,0,3,2,1:T(8,128)}), f32[4,2,2,8,8,128]{5,4,0,3,2,1:T(8,128)S(1)}, u32[]{:S(2)}, u32[]{:S(2)}) async-start(f32[4,2,2,8,8,128]{5,4,0,3,2,1:T(8,128)} %bitcast.27), calls=%async_computation.2 | async-start | bytes 1048576 | tf_op jit(solution)/shard_map/all_to_all | solution.py:135
Sparse Core Ops, SparseCore 0:
  9.5 44.1 all-gather.2
where the time goes:
time: 198 us; the launch traced here: 197 us
  other arithmetic  47.7 us (24%)
  blocking collectives  45.5 us (23%)
  local copies, waits for them, and re-layouts  36 us (18%)
  starting transfers between devices  20.9 us (11%)
  waiting for transfers between devices  17.1 us (9%)
  between operations  15.1 us (8%)
  matrix products  15 us (8%)
    unnamed x1, other arithmetic  45.2 us
    unnamed x36, local copies, waits for them, and re-layouts  27.6 us
    all_gather x1, blocking collectives, body(): lax.all_gather(shrink.reshape(steps, slots, adapter_rank), 'ada', axis=1,...  19 us
    squeeze x1, blocking collectives, body(): row_adapter = group_ids[:, 0]  12.3 us
    all_to_all x1, starting transfers between devices, body(): lax.all_to_all(adapter_up, 'ada', split_axis=2, concat_axis=0, tiled=True)  7.42 us
    all_to_all x1, waiting for transfers between devices, body(): lax.all_to_all(query_columns, 'ada', split_axis=1, concat_axis=2, tiled=T...  6.79 us
    dot_general x1, matrix products, body(): jnp.dot(whole_inputs.reshape(steps * group, width), query_weight, preferr...  5.7 us
    all_to_all x1, waiting for transfers between devices, body(): lax.all_to_all(partial_numerator, 'dec', split_axis=1, concat_axis=1, til...  5.68 us
  transfers between devices with their start and end apart: 6, of which 4 were waited for; matrix products, arithmetic and copies ran while one was open for 40% of the time, Pallas kernels for 0%

commit v1 on v0

--- a/solution.py
+++ b/solution.py
@@ -10,6 +10,29 @@
 CAP = 4
 NEGATIVE = -1e30
 HIGH = lax.Precision.HIGHEST
+
+
+def in_blocks(array, dim, size):
+    shape = array.shape
+    parts = array.reshape(*shape[:dim], size, shape[dim] // size, *shape[dim + 1 :])
+    return jnp.moveaxis(parts, dim, 0)
+
+
+def joined_along(blocks, dim):
+    blocks = jnp.moveaxis(blocks, 0, dim)
+    lengths = blocks.shape
+    return blocks.reshape(*lengths[:dim], lengths[dim] * lengths[dim + 1], *lengths[dim + 2 :])
+
+
+def pairwise_exchange(x, axis, split_dim, concat_dim):
+    devices, index = (lax.axis_size(axis), lax.axis_index(axis))
+    parts = in_blocks(x, split_dim, devices)
+    finished = [parts[index]]
+    for step in range(1, devices):
+        sent = parts[index ^ step]
+        finished.append(lax.ppermute(sent, axis, [(i, i ^ step) for i in range(devices)]))
+    parts = jnp.stack(finished)[index ^ jnp.arange(devices)]
+    return joined_along(parts, concat_dim)
 
 
 def cache_part(query, keys, values, live):
@@ -107,7 +130,7 @@
         "mr,urx->umx", slot_position, received_rows, preferred_element_type=jnp.float32
     )
     query_columns = (base_output + low_rank_update).astype(jnp.bfloat16)
-    query_local = lax.all_to_all(query_columns, "ada", split_axis=1, concat_axis=2, tiled=True)
+    query_local = pairwise_exchange(query_columns, "ada", 1, 2)
     group_heads = HEADS // KVH
     query = query_local.reshape(steps, row_local, KVH, group_heads, HD)
     fresh = fresh_part(query, new_cache)

time: 198 us -> 214 us (1.081)
  starting transfers between devices: 20.9 us -> 38.4 us
  waiting for transfers between devices: 17.1 us -> 12.3 us
  blocking collectives: 45.5 us -> 48.2 us
    ppermute x0 -> x15, starting transfers between devices: none -> 21.1 us  [pairwise_exchange(): lax.ppermute(sent, axis, [(i, i ^ step) for i in range(devices)])]
    all_to_all x1 -> x0, waiting for transfers between devices: 6.79 us -> none  [body(): lax.all_to_all(query_columns, 'ada', split_axis=1, concat_axis=2, tiled=T...]
    all_to_all x1 -> x0, starting transfers between devices: 3.51 us -> none  [body(): lax.all_to_all(query_columns, 'ada', split_axis=1, concat_axis=2, tiled=T...]
    unnamed x36 -> x53, local copies, waits for them, and re-layouts: 27.6 us -> 27.2 us
  transfers between devices with their start and end apart: 6 -> 20, of which waited for: 4 -> 4; matrix products, arithmetic and copies ran while one was open for 40% -> 37% of each run, Pallas kernels for 0% -> 0%
where the time goes in v1:
time: 214 us; the launch traced here: 213 us
  blocking collectives  48.2 us (23%)
  other arithmetic  47.7 us (22%)
  starting transfers between devices  38.4 us (18%)
  local copies, waits for them, and re-layouts  35.5 us (17%)
  between operations  15.5 us (7%)
  matrix products  15 us (7%)
  waiting for transfers between devices  12.3 us (6%)
    unnamed x1, other arithmetic  45.2 us
    unnamed x53, local copies, waits for them, and re-layouts  27.2 us
    ppermute x15, starting transfers between devices, pairwise_exchange(): lax.ppermute(sent, axis, [(i, i ^ step) for i in range(devices)])  21.1 us
    all_gather x1, blocking collectives, body(): lax.all_gather(shrink.reshape(steps, slots, adapter_rank), 'ada', axis=1,...  19.6 us
    squeeze x1, blocking collectives, body(): row_adapter = group_ids[:, 0]  13.9 us
    all_to_all x1, starting transfers between devices, body(): lax.all_to_all(adapter_up, 'ada', split_axis=2, concat_axis=0, tiled=True)  7.42 us
    all_gather x1, blocking collectives, body(): lax.all_gather(query_local, 'dec', axis=1, tiled=True)  6.16 us
    dot_general x1, matrix products, body(): jnp.dot(whole_inputs.reshape(steps * group, width), query_weight, preferr...  5.69 us
  transfers between devices with their start and end apart: 20, of which 4 were waited for; matrix products, arithmetic and copies ran while one was open for 37% of the time, Pallas kernels for 0%

profile of v1, /device:TPU:0, one launch (start us, length us, event | category | flops | bytes accessed | tf_op | source)
XLA Modules:
  0.0 212.5 jit_solution(9076290997978294312)
XLA Ops:
  6.5 1.8 copy.135
  8.3 9.2 %copy.140 = bf16[1,64,8192]{1,0,2:T(2,128)(2,1)} copy(bf16[1,64,8192]{2,1,0:T(8,128)(2,1)} %param.12) | data formatting | bytes 2097152 | tf_op args[3]
  17.5 0.5 broadcast.195
  18.0 45.2 %reduce.4 = bf16[8192,64]{1,0:T(8,128)(2,1)S(1)} reduce(bf16[8192,1,64]{2,1,0:T(2,128)(2,1)} %bitcast.193, bf16[]{:T(256)} %broadcast.195), dimensions={1}, to_apply=%bitcast.161.reduce_sub_computation | reduce | bytes 2097154
  63.2 2.3 %reshape.223 = bf16[16,2,16384]{2,1,0:T(2,128)(2,1)} reshape(bf16[8192,64]{1,0:T(8,128)(2,1)S(1)} %reduce.4) | data formatting | bytes 2097152
  65.5 0.7 dynamic-slice.64
  66.9 0.2 dynamic-update-slice
  67.1 7.4 %all-to-all-start = ((bf16[16,2,16384]{2,1,0:T(2,128)(2,1)}), bf16[16,2,16384]{2,1,0:T(2,128)(2,1)S(1)}, u32[]{:S(2)}, u32[]{:S(2)}) async-start(bf16[16,2,16384]{2,1,0:T(2,128)(2,1)} %reshape.223), calls=%async_computation | async-start | bytes 2097152 | tf_op jit(solution)/shard_map/all_to_all | solution.py:115
  74.5 4.3 %all-reduce = s32[4]{0:T(128)S(1)} all-reduce(s32[4]{0:T(128)S(1)} %dynamic-update-slice), channel_id=1, replica_groups=mesh['dec'=2,'ada'=16] {'dec'}, use_global_device_ids=true, to_apply=%add | all-reduce | flops 4 | bytes 32
  78.8 4.2 %all-gather = s32[2,2,4]{2,1,0:T(2,128)S(1)} all-gather(s32[1,2,4]{2,1,0:T(2,128)S(1)} %bitcast.233), channel_id=1, replica_groups=mesh['dec'=2,'ada'=16] {'dec'}, dimensions={0}, use_global_device_ids=true | all-gather | bytes 96 | tf_op jit(solution)/shard_map/all_gather | solution.py:143
  83.1 0.7 dynamic-slice.65
  84.7 0.2 slice_reduce_fusion
  84.9 1.7 gather_fusion
  86.6 0.1 fusion.56
  86.7 0.1 copy.199
  87.0 0.2 copy-done.7
  87.3 13.9 %all-reduce.1 = s32[32]{0:T(128)S(1)} all-reduce(s32[32]{0:T(128)S(1)} %bitcast_dynamic-update-slice_fusion), channel_id=1, replica_groups=mesh['dec'=2,'ada'=16] {'ada'}, use_global_device_ids=true, to_apply=%add.1 | all-reduce | flops 32 | bytes 256 | tf_op jit(solution)/shard_map/squeeze | solution.py:97
  101.3 0.2 convert_reduce_fusion
  101.5 0.9 bitcast_bitcast_fusion
  102.4 0.8 bitcast_bitcast_fusion.1
  103.2 7.0 %reshape.224 = bf16[8192,1,64]{2,1,0:T(2,128)(2,1)} reshape(bf16[16,2,16384]{2,1,0:T(2,128)(2,1)S(1)} %all-to-all-done) | data formatting | bytes 2097152
  110.2 2.5 %copy.194 = bf16[1,64,8192]{1,2,0:T(8,128)(2,1)S(1)} copy(bf16[1,64,8192]{1,0,2:T(2,128)(2,1)} %bitcast.194) | data formatting | bytes 2097152
  112.7 1.6 copy.142
  114.4 4.4 %fusion.19 = bf16[4,4,64]{2,1,0:T(4,128)(2,1)S(1)} fusion(bf16[4,32,8192]{2,0,1:T(4,128)(2,1)} %all-gather.3.cloned.1.call-done, bf16[1,8192,64]{1,2,0:T(8,128)(2,1)S(1)} %copy-done, s32[32]{0:T(128)S(1)} %get-tuple-element.11), kind=kOutput, calls=%fused_computation.25 | convolution fusion | flops 25298048 | bytes 3147904 | tf_op jit(solution)/shard_map/tjcd,jdr->tjcr/dot_general | solution.py:112
  118.7 19.6 %all_gather.22 = bf16[4,64,64]{2,0,1:T(4,128)(2,1)S(1)} all-gather(bf16[4,4,64]{2,0,1:T(4,128)(2,1)S(1)} %copy.138), channel_id=1, replica_groups=mesh['dec'=2,'ada'=16] {'ada'}, dimensions={1}, use_global_device_ids=true | all-gather | bytes 34816 | tf_op jit(solution)/shard_map/all_gather | solution.py:116
  138.4 1.5 fusion.7
  139.8 0.1 copy.144
  140.0 5.7 %fusion.1 = f32[4,32,512]{2,1,0:T(8,128)S(1)} fusion(bf16[8192,512]{1,0:T(8,128)(2,1)} %param.10, bf16[4,32,8192]{2,0,1:T(4,128)(2,1)S(1)} %copy-done.1), kind=kOutput, calls=%fused_computation.4 | convolution fusion | flops 1073741824 | bytes 10747904 | tf_op jit(solution)/shard_map/dot_general | solution.py:93
  145.7 0.2 fusion.15
  146.0 0.2 constant_dynamic-slice_fusion
  146.2 0.4 collective-permute-start
  146.6 1.5 collective-permute-start.2
  148.1 2.0 collective-permute-start.4
  150.4 2.4 %collective-permute-start.6 = (bf16[4,2,512]{2,0,1:T(4,128)(2,1)S(1)}, bf16[4,2,512]{2,0,1:T(4,128)(2,1)S(1)}, u32[]{:S(2)}, u32[]{:S(2)}) collective-permute-start(bf16[4,2,512]{2,0,1:T(4,128)(2,1)S(1)} %bitcast.229), channel_id=1, source_target_pairs={{0,7},{1,6},{2,5},{3,4},{4,3},{5,2},{6,1},{7,0},{8,15},{9,14},{10,... | collective-permute-start | bytes 24584 | tf_op jit(solution)/shard_map/ppermute | solution.py:33
  152.9 2.9 %collective-permute-start.8 = (bf16[4,2,512]{2,0,1:T(4,128)(2,1)S(1)}, bf16[4,2,512]{2,0,1:T(4,128)(2,1)S(1)}, u32[]{:S(2)}, u32[]{:S(2)}) collective-permute-start(bf16[4,2,512]{2,0,1:T(4,128)(2,1)S(1)} %bitcast.225), channel_id=1, source_target_pairs={{0,9},{1,8},{2,11},{3,10},{4,13},{5,12},{6,15},{7,14},{8,1},{9,0},... | collective-permute-start | bytes 24584 | tf_op jit(solution)/shard_map/ppermute | solution.py:33
  156.0 3.3 %collective-permute-start.10 = (bf16[4,2,512]{2,0,1:T(4,128)(2,1)S(1)}, bf16[4,2,512]{2,0,1:T(4,128)(2,1)S(1)}, u32[]{:S(2)}, u32[]{:S(2)}) collective-permute-start(bf16[4,2,512]{2,0,1:T(4,128)(2,1)S(1)} %bitcast.222), channel_id=1, source_target_pairs={{0,11},{1,10},{2,9},{3,8},{4,15},{5,14},{6,13},{7,12},{8,3},{9,2},... | collective-permute-start | bytes 24584 | tf_op jit(solution)/shard_map/ppermute | solution.py:33
  159.4 3.8 %collective-permute-start.12 = (bf16[4,2,512]{2,0,1:T(4,128)(2,1)S(1)}, bf16[4,2,512]{2,0,1:T(4,128)(2,1)S(1)}, u32[]{:S(2)}, u32[]{:S(2)}) collective-permute-start(bf16[4,2,512]{2,0,1:T(4,128)(2,1)S(1)} %bitcast.220), channel_id=1, source_target_pairs={{0,13},{1,12},{2,15},{3,14},{4,9},{5,8},{6,11},{7,10},{8,5},{9,4},... | collective-permute-start | bytes 24584 | tf_op jit(solution)/shard_map/ppermute | solution.py:33
  163.3 0.1 collective-permute-start.13
  163.4 4.2 %collective-permute-start.14 = (bf16[4,2,512]{2,0,1:T(4,128)(2,1)S(1)}, bf16[4,2,512]{2,0,1:T(4,128)(2,1)S(1)}, u32[]{:S(2)}, u32[]{:S(2)}) collective-permute-start(bf16[4,2,512]{2,0,1:T(4,128)(2,1)S(1)} %bitcast.218), channel_id=1, source_target_pairs={{0,15},{1,14},{2,13},{3,12},{4,11},{5,10},{6,9},{7,8},{8,7},{9,6},... | collective-permute-start | bytes 24584 | tf_op jit(solution)/shard_map/ppermute | solution.py:33
  167.7 2.0 collective-permute-done.13
  169.7 0.7 gather_fusion.1
  170.6 6.2 %all_gather.23 = bf16[4,4,8192]{2,0,1:T(4,128)(2,1)S(1)} all-gather(bf16[4,2,8192]{2,0,1:T(4,128)(2,1)S(1)} %bitcast.204), channel_id=1, replica_groups=mesh['dec'=2,'ada'=16] {'dec'}, dimensions={1}, use_global_device_ids=true | all-gather | bytes 393216 | tf_op jit(solution)/shard_map/all_gather | solution.py:142
  176.7 0.3 reshape.220
  177.0 0.5 fusion.57
  177.5 0.4 fusion.27
  178.0 1.5 fusion.25
  179.4 0.7 reshape.225
  180.2 3.2 %all-to-all-start.2 = ((f32[2,1,512]{2,1,0:T(1,128)}), f32[2,1,512]{2,1,0:T(1,128)S(1)}, u32[]{:S(2)}, u32[]{:S(2)}) async-start(f32[2,1,512]{2,1,0:T(1,128)} %reshape.225), calls=%async_computation.2 | async-start | bytes 8192 | tf_op jit(solution)/shard_map/all_to_all | solution.py:159
  183.4 0.7 fusion.58
  184.1 0.2 fusion.34
  184.3 0.7 reshape.227
  185.0 2.2 %all-to-all-done.2 = f32[2,1,512]{2,1,0:T(1,128)S(1)} async-done(((f32[2,1,512]{2,1,0:T(1,128)}), f32[2,1,512]{2,1,0:T(1,128)S(1)}, u32[]{:S(2)}, u32[]{:S(2)}) %all-to-all-start.2) | async-done | bytes 4128 | tf_op jit(solution)/shard_map/all_to_all | solution.py:159
  187.2 3.2 %all-to-all-start.3 = ((f32[2,1,512]{2,1,0:T(1,128)}), f32[2,1,512]{2,1,0:T(1,128)S(1)}, u32[]{:S(2)}, u32[]{:S(2)}) async-start(f32[2,1,512]{2,1,0:T(1,128)} %reshape.227), calls=%async_computation.3 | async-start | bytes 8192 | tf_op jit(solution)/shard_map/all_to_all | solution.py:160
  190.4 0.5 broadcast.196
  190.9 0.7 reduce.5
  191.6 0.1 reshape.226
  191.8 2.4 %all-to-all-done.3 = f32[2,1,512]{2,1,0:T(1,128)S(1)} async-done(((f32[2,1,512]{2,1,0:T(1,128)}), f32[2,1,512]{2,1,0:T(1,128)S(1)}, u32[]{:S(2)}, u32[]{:S(2)}) %all-to-all-start.3) | async-done | bytes 4128 | tf_op jit(solution)/shard_map/all_to_all | solution.py:160
  194.2 3.5 %all-to-all-start.1 = ((f32[4,2,2,8,8,128]{5,4,0,3,2,1:T(8,128)}), f32[4,2,2,8,8,128]{5,4,0,3,2,1:T(8,128)S(1)}, u32[]{:S(2)}, u32[]{:S(2)}) async-start(f32[4,2,2,8,8,128]{5,4,0,3,2,1:T(8,128)} %bitcast.57), calls=%async_computation.1 | async-start | bytes 1048576 | tf_op jit(solution)/shard_map/all_to_all | solution.py:158
  197.7 0.7 reduce.6
  198.3 0.1 reshape.228
  198.5 5.7 %all-to-all-done.1 = f32[4,2,2,8,8,128]{5,4,0,3,2,1:T(8,128)S(1)} async-done(((f32[4,2,2,8,8,128]{5,4,0,3,2,1:T(8,128)}), f32[4,2,2,8,8,128]{5,4,0,3,2,1:T(8,128)S(1)}, u32[]{:S(2)}, u32[]{:S(2)}) %all-to-all-start.1) | async-done | bytes 524320 | tf_op jit(solution)/shard_map/all_to_all | solution.py:158
  204.2 0.2 multiply_reduce_fusion
  204.4 0.5 fusion.16
  205.0 0.7 reshape.173
  (101 shorter events, 1.6 us)
Async XLA Ops:
  6.5 107.8 %copy-start = (bf16[1,8192,64]{1,2,0:T(8,128)(2,1)S(1)}, bf16[1,8192,64]{1,2,0:T(8,128)(2,1)}, u32[]{:S(2)}) copy-start(bf16[1,8192,64]{1,2,0:T(8,128)(2,1)} %param.11) | copy-start | bytes 3145732
  6.5 107.8 %all-gather.3.cloned.1.call-start = ((), (), s32[]{:S(2)}) async-start(), calls=%async_computation.4 | async-start | bytes 2228224 | tf_op jit(solution)/shard_map/all_gather | solution.py:90
  63.2 2.3 %copy-start.9 = (u32[32]{0:T(128)S(1)}, u32[32]{0:T(128)}, u32[]{:S(2)}) copy-start(u32[32]{0:T(128)} %constant.114) | copy-start | bytes 388
  63.2 3.7 %copy-start.6 = (s32[2]{0:T(128)S(1)}, s32[2]{0:T(128)}, u32[]{:S(2)}) copy-start(s32[2]{0:T(128)} %param.17) | copy-start | bytes 28
  63.2 15.6 %copy-start.5 = (s32[2,4]{1,0:T(2,128)S(1)}, s32[2,4]{1,0:T(2,128)}, u32[]{:S(2)}) copy-start(s32[2,4]{1,0:T(2,128)} %param.16) | copy-start | bytes 100
  63.2 19.9 %copy-start.8 = (u32[32]{0:T(128)S(1)}, u32[32]{0:T(128)}, u32[]{:S(2)}) copy-start(u32[32]{0:T(128)} %constant.119) | copy-start | bytes 388
  63.2 21.5 %copy-start.4 = (bf16[4,2,2,1024]{3,2,1,0:T(2,128)(2,1)S(1)}, bf16[4,2,2,1024]{3,2,1,0:T(2,128)(2,1)}, u32[]{:S(2)}) copy-start(bf16[4,2,2,1024]{3,2,1,0:T(2,128)(2,1)} %param.14) | copy-start | bytes 98308
  67.1 36.1 %all-to-all-start = ((bf16[16,2,16384]{2,1,0:T(2,128)(2,1)}), bf16[16,2,16384]{2,1,0:T(2,128)(2,1)S(1)}, u32[]{:S(2)}, u32[]{:S(2)}) async-start(bf16[16,2,16384]{2,1,0:T(2,128)(2,1)} %reshape.223), calls=%async_computation | async-start | bytes 2097152 | tf_op jit(solution)/shard_map/all_to_all | solution.py:115
  86.6 0.7 copy-start.7
  114.3 25.6 %copy-start.1 = (bf16[4,32,8192]{2,0,1:T(4,128)(2,1)S(1)}, bf16[4,32,8192]{2,0,1:T(4,128)(2,1)}, u32[]{:S(2)}) copy-start(bf16[4,32,8192]{2,0,1:T(4,128)(2,1)} %all-gather.3.cloned.1.call-done) | copy-start | bytes 6291460
  145.7 31.4 %copy-start.3 = (bf16[4,64,8,128,1]{3,2,1,0,4:T(8,128)(2,1)S(1)}, bf16[4,64,8,128,1]{3,2,1,0,4:T(8,128)(2,1)}, u32[]{:S(2)}) copy-start(bf16[4,64,8,128,1]{3,2,1,0,4:T(8,128)(2,1)} %bitcast_bitcast_fusion) | copy-start | bytes 1572868
  146.2 4.0 %collective-permute-start = (bf16[4,2,512]{2,0,1:T(4,128)(2,1)S(1)}, bf16[4,2,512]{2,0,1:T(4,128)(2,1)S(1)}, u32[]{:S(2)}, u32[]{:S(2)}) collective-permute-start(bf16[4,2,512]{2,0,1:T(4,128)(2,1)S(1)} %bitcast.232), channel_id=1, source_target_pairs={{0,1},{1,0},{2,3},{3,2},{4,5},{5,4},{6,7},{7,6},{8,9},{9,8},{10,11... | collective-permute-start | bytes 24584 | tf_op jit(solution)/shard_map/ppermute | solution.py:33
  146.6 3.7 %collective-permute-start.1 = (bf16[4,2,512]{2,0,1:T(4,128)(2,1)S(1)}, bf16[4,2,512]{2,0,1:T(4,128)(2,1)S(1)}, u32[]{:S(2)}, u32[]{:S(2)}) collective-permute-start(bf16[4,2,512]{2,0,1:T(4,128)(2,1)S(1)} %bitcast.230), channel_id=1, source_target_pairs={{0,2},{1,3},{2,0},{3,1},{4,6},{5,7},{6,4},{7,5},{8,10},{9,11},{10,... | collective-permute-start | bytes 24584 | tf_op jit(solution)/shard_map/ppermute | solution.py:33
  146.6 6.2 %collective-permute-start.2 = (bf16[4,2,512]{2,0,1:T(4,128)(2,1)S(1)}, bf16[4,2,512]{2,0,1:T(4,128)(2,1)S(1)}, u32[]{:S(2)}, u32[]{:S(2)}) collective-permute-start(bf16[4,2,512]{2,0,1:T(4,128)(2,1)S(1)} %bitcast.228), channel_id=1, source_target_pairs={{0,3},{1,2},{2,1},{3,0},{4,7},{5,6},{6,5},{7,4},{8,11},{9,10},{10,... | collective-permute-start | bytes 24584 | tf_op jit(solution)/shard_map/ppermute | solution.py:33
  148.1 4.8 %collective-permute-start.3 = (bf16[4,2,512]{2,0,1:T(4,128)(2,1)S(1)}, bf16[4,2,512]{2,0,1:T(4,128)(2,1)S(1)}, u32[]{:S(2)}, u32[]{:S(2)}) collective-permute-start(bf16[4,2,512]{2,0,1:T(4,128)(2,1)S(1)} %bitcast.226), channel_id=1, source_target_pairs={{0,4},{1,5},{2,6},{3,7},{4,0},{5,1},{6,2},{7,3},{8,12},{9,13},{10,... | collective-permute-start | bytes 24584 | tf_op jit(solution)/shard_map/ppermute | solution.py:33
  148.1 7.7 %collective-permute-start.4 = (bf16[4,2,512]{2,0,1:T(4,128)(2,1)S(1)}, bf16[4,2,512]{2,0,1:T(4,128)(2,1)S(1)}, u32[]{:S(2)}, u32[]{:S(2)}) collective-permute-start(bf16[4,2,512]{2,0,1:T(4,128)(2,1)S(1)} %bitcast.224), channel_id=1, source_target_pairs={{0,5},{1,4},{2,7},{3,6},{4,1},{5,0},{6,3},{7,2},{8,13},{9,12},{10,... | collective-permute-start | bytes 24584 | tf_op jit(solution)/shard_map/ppermute | solution.py:33
  150.3 5.7 %collective-permute-start.5 = (bf16[4,2,512]{2,0,1:T(4,128)(2,1)S(1)}, bf16[4,2,512]{2,0,1:T(4,128)(2,1)S(1)}, u32[]{:S(2)}, u32[]{:S(2)}) collective-permute-start(bf16[4,2,512]{2,0,1:T(4,128)(2,1)S(1)} %bitcast.231), channel_id=1, source_target_pairs={{0,6},{1,7},{2,4},{3,5},{4,2},{5,3},{6,0},{7,1},{8,14},{9,15},{10,... | collective-permute-start | bytes 24584 | tf_op jit(solution)/shard_map/ppermute | solution.py:33
  150.4 9.0 %collective-permute-start.6 = (bf16[4,2,512]{2,0,1:T(4,128)(2,1)S(1)}, bf16[4,2,512]{2,0,1:T(4,128)(2,1)S(1)}, u32[]{:S(2)}, u32[]{:S(2)}) collective-permute-start(bf16[4,2,512]{2,0,1:T(4,128)(2,1)S(1)} %bitcast.229), channel_id=1, source_target_pairs={{0,7},{1,6},{2,5},{3,4},{4,3},{5,2},{6,1},{7,0},{8,15},{9,14},{10,... | collective-permute-start | bytes 24584 | tf_op jit(solution)/shard_map/ppermute | solution.py:33
  152.8 6.6 %collective-permute-start.7 = (bf16[4,2,512]{2,0,1:T(4,128)(2,1)S(1)}, bf16[4,2,512]{2,0,1:T(4,128)(2,1)S(1)}, u32[]{:S(2)}, u32[]{:S(2)}) collective-permute-start(bf16[4,2,512]{2,0,1:T(4,128)(2,1)S(1)} %bitcast.227), channel_id=1, source_target_pairs={{0,8},{1,9},{2,10},{3,11},{4,12},{5,13},{6,14},{7,15},{8,0},{9,1},... | collective-permute-start | bytes 24584 | tf_op jit(solution)/shard_map/ppermute | solution.py:33
  152.9 10.3 %collective-permute-start.8 = (bf16[4,2,512]{2,0,1:T(4,128)(2,1)S(1)}, bf16[4,2,512]{2,0,1:T(4,128)(2,1)S(1)}, u32[]{:S(2)}, u32[]{:S(2)}) collective-permute-start(bf16[4,2,512]{2,0,1:T(4,128)(2,1)S(1)} %bitcast.225), channel_id=1, source_target_pairs={{0,9},{1,8},{2,11},{3,10},{4,13},{5,12},{6,15},{7,14},{8,1},{9,0},... | collective-permute-start | bytes 24584 | tf_op jit(solution)/shard_map/ppermute | solution.py:33
  155.9 7.5 %collective-permute-start.9 = (bf16[4,2,512]{2,0,1:T(4,128)(2,1)S(1)}, bf16[4,2,512]{2,0,1:T(4,128)(2,1)S(1)}, u32[]{:S(2)}, u32[]{:S(2)}) collective-permute-start(bf16[4,2,512]{2,0,1:T(4,128)(2,1)S(1)} %bitcast.223), channel_id=1, source_target_pairs={{0,10},{1,11},{2,8},{3,9},{4,14},{5,15},{6,12},{7,13},{8,2},{9,3},... | collective-permute-start | bytes 24584 | tf_op jit(solution)/shard_map/ppermute | solution.py:33
  156.0 11.7 %collective-permute-start.10 = (bf16[4,2,512]{2,0,1:T(4,128)(2,1)S(1)}, bf16[4,2,512]{2,0,1:T(4,128)(2,1)S(1)}, u32[]{:S(2)}, u32[]{:S(2)}) collective-permute-start(bf16[4,2,512]{2,0,1:T(4,128)(2,1)S(1)} %bitcast.222), channel_id=1, source_target_pairs={{0,11},{1,10},{2,9},{3,8},{4,15},{5,14},{6,13},{7,12},{8,3},{9,2},... | collective-permute-start | bytes 24584 | tf_op jit(solution)/shard_map/ppermute | solution.py:33
  159.3 8.3 %collective-permute-start.11 = (bf16[4,2,512]{2,0,1:T(4,128)(2,1)S(1)}, bf16[4,2,512]{2,0,1:T(4,128)(2,1)S(1)}, u32[]{:S(2)}, u32[]{:S(2)}) collective-permute-start(bf16[4,2,512]{2,0,1:T(4,128)(2,1)S(1)} %bitcast.221), channel_id=1, source_target_pairs={{0,12},{1,13},{2,14},{3,15},{4,8},{5,9},{6,10},{7,11},{8,4},{9,5},... | collective-permute-start | bytes 24584 | tf_op jit(solution)/shard_map/ppermute | solution.py:33
  159.4 8.2 %collective-permute-start.12 = (bf16[4,2,512]{2,0,1:T(4,128)(2,1)S(1)}, bf16[4,2,512]{2,0,1:T(4,128)(2,1)S(1)}, u32[]{:S(2)}, u32[]{:S(2)}) collective-permute-start(bf16[4,2,512]{2,0,1:T(4,128)(2,1)S(1)} %bitcast.220), channel_id=1, source_target_pairs={{0,13},{1,12},{2,15},{3,14},{4,9},{5,8},{6,11},{7,10},{8,5},{9,4},... | collective-permute-start | bytes 24584 | tf_op jit(solution)/shard_map/ppermute | solution.py:33
  163.3 6.4 %collective-permute-start.13 = (bf16[4,2,512]{2,0,1:T(4,128)(2,1)S(1)}, bf16[4,2,512]{2,0,1:T(4,128)(2,1)S(1)}, u32[]{:S(2)}, u32[]{:S(2)}) collective-permute-start(bf16[4,2,512]{2,0,1:T(4,128)(2,1)S(1)} %bitcast.219), channel_id=1, source_target_pairs={{0,14},{1,15},{2,12},{3,13},{4,10},{5,11},{6,8},{7,9},{8,6},{9,7},... | collective-permute-start | bytes 24584 | tf_op jit(solution)/shard_map/ppermute | solution.py:33
  163.4 6.3 %collective-permute-start.14 = (bf16[4,2,512]{2,0,1:T(4,128)(2,1)S(1)}, bf16[4,2,512]{2,0,1:T(4,128)(2,1)S(1)}, u32[]{:S(2)}, u32[]{:S(2)}) collective-permute-start(bf16[4,2,512]{2,0,1:T(4,128)(2,1)S(1)} %bitcast.218), channel_id=1, source_target_pairs={{0,15},{1,14},{2,13},{3,12},{4,11},{5,10},{6,9},{7,8},{8,7},{9,6},... | collective-permute-start | bytes 24584 | tf_op jit(solution)/shard_map/ppermute | solution.py:33
  167.6 10.3 %copy-start.2 = (bf16[4,64,8,128,1]{3,2,1,0,4:T(8,128)(2,1)S(1)}, bf16[4,64,8,128,1]{3,2,1,0,4:T(8,128)(2,1)}, u32[]{:S(2)}) copy-start(bf16[4,64,8,128,1]{3,2,1,0,4:T(8,128)(2,1)} %bitcast_bitcast_fusion.1) | copy-start | bytes 1572868
  180.2 7.0 %all-to-all-start.2 = ((f32[2,1,512]{2,1,0:T(1,128)}), f32[2,1,512]{2,1,0:T(1,128)S(1)}, u32[]{:S(2)}, u32[]{:S(2)}) async-start(f32[2,1,512]{2,1,0:T(1,128)} %reshape.225), calls=%async_computation.2 | async-start | bytes 8192 | tf_op jit(solution)/shard_map/all_to_all | solution.py:159
  187.2 7.0 %all-to-all-start.3 = ((f32[2,1,512]{2,1,0:T(1,128)}), f32[2,1,512]{2,1,0:T(1,128)S(1)}, u32[]{:S(2)}, u32[]{:S(2)}) async-start(f32[2,1,512]{2,1,0:T(1,128)} %reshape.227), calls=%async_computation.3 | async-start | bytes 8192 | tf_op jit(solution)/shard_map/all_to_all | solution.py:160
  194.2 10.1 %all-to-all-start.1 = ((f32[4,2,2,8,8,128]{5,4,0,3,2,1:T(8,128)}), f32[4,2,2,8,8,128]{5,4,0,3,2,1:T(8,128)S(1)}, u32[]{:S(2)}, u32[]{:S(2)}) async-start(f32[4,2,2,8,8,128]{5,4,0,3,2,1:T(8,128)} %bitcast.57), calls=%async_computation.1 | async-start | bytes 1048576 | tf_op jit(solution)/shard_map/all_to_all | solution.py:158
Sparse Core Ops, SparseCore 0:
  9.5 44.1 all-gather.2
